TPU v7x, 32 devices: a whole 2x2x4 slice. The times are simulated.
32 devices in a mesh: dp: 4 (over y, x), seq: 2 (over core), tensor: 4 (over z).
Axes of the slice: x: 2, y: 2, z: 4, core: 2. Of those that a mesh axis runs over, the one named last changes fastest.
Arguments:
- block_input: float32 [4, 16, 256, 1024], P('dp', 'seq', 'tensor'), may hold values from -6 to 6
- w_qkv: bfloat16 [1024, 3, 1024], P(None, None, 'tensor'), may hold values from -0.1875 to 0.1875
- qv_bias: bfloat16 [2, 1024], P(None, 'tensor'), may hold values from -3 to 3
- w_out: bfloat16 [1024, 1024], P('tensor'), may hold values from -3 to 3
- b_out: bfloat16 [1024], replicated, may hold values from -3 to 3
- w_up: bfloat16 [1024, 4096], P(None, 'tensor'), may hold values from -0.1875 to 0.1875
- b_up: bfloat16 [4096], P('tensor'), may hold values from -3 to 3
- w_down: bfloat16 [4096, 1024], P('tensor'), may hold values from -0.09375 to 0.09375
- b_down: bfloat16 [1024], replicated, may hold values from -3 to 3
- w_mod: bfloat16 [1024, 6144], replicated, may hold values from -0.375 to 0.375
- b_mod: bfloat16 [6144], replicated, may hold values from -3 to 3
- context_frames: int32 [4], P('dp'), may hold values from 1 to 15
- noise_levels: int32 [4, 16], P('dp', 'seq'), may hold values from 0 to 999
- cotangent: float32 [4, 16, 256, 1024], P('dp', 'seq', 'tensor'), may hold values from -6 to 6
Outputs:
- output: float32 [4, 16, 256, 1024], P('dp', 'seq', 'tensor')
- grad_input: float32 [4, 16, 256, 1024], P('dp', 'seq', 'tensor')
- grad_w_qkv: float32 [1024, 3, 1024], P(None, None, 'tensor')
- grad_qv_bias: float32 [2, 1024], P(None, 'tensor')
- grad_w_out: float32 [1024, 1024], P('tensor')
- grad_b_out: float32 [1024], P('tensor')
- grad_w_up: float32 [1024, 4096], P(None, 'tensor')
- grad_b_up: float32 [4096], P('tensor')
- grad_w_down: float32 [4096, 1024], P('tensor')
- grad_b_down: float32 [1024], P('tensor')
- grad_w_mod: float32 [1024, 6144], P(None, 'tensor')
- grad_b_mod: float32 [6144], P('tensor')
Inputs may be any that keep to these rules, and one draw needn't show every extreme that they name: `noise_levels`: noise level index of each frame.
All inputs are finite; a program needn't handle non-finite values.
Results may differ from a plain program's by a relative error of at most 0.02.
Values may be sent and summed in bfloat16 or wider, within the bound.
No kernel may reach another device: no remote copies, remote signals or barrier semaphores. Data moves between devices by JAX's collectives and lax.ppermute only.
A program may use at most 256 MiB of HBM per device.

v0:
```python
import math

import jax
import jax.numpy as jnp
from jax import lax
from jax.sharding import PartitionSpec as P

HD = 64


def level_features(levels, context, frame_ids, breadth):
    level_used = jnp.where(frame_ids[None, :] < context[:, None], 0, levels).astype(jnp.float32)
    halfway = breadth // 2
    frequency = jnp.exp(-math.log(10000.0) * jnp.arange(halfway, dtype=jnp.float32) / halfway)
    angles = level_used[..., None] * frequency
    return jax.nn.silu(jnp.concatenate([jnp.cos(angles), jnp.sin(angles)], axis=-1))


def normalize(stream):
    centre = stream - jnp.mean(stream, axis=-1, keepdims=True)
    inverse = lax.rsqrt(jnp.mean(centre * centre, axis=-1, keepdims=True) + 1e-06)
    return (centre * inverse, inverse)


def norm_back(grad_normed, normed, inverse):
    first_mean = jnp.mean(grad_normed, axis=-1, keepdims=True)
    second_mean = jnp.mean(grad_normed * normed, axis=-1, keepdims=True)
    return inverse * (grad_normed - first_mean - normed * second_mean)


def gelu_back(pre_act, grad_act):
    _, pullback = jax.vjp(lambda argument: jax.nn.gelu(argument, approximate=True), pre_act)
    return pullback(grad_act)[0]


def body(
    block_input,
    w_qkv,
    qv_bias,
    w_out,
    b_out,
    w_up,
    b_up,
    w_down,
    b_down,
    w_mod,
    b_mod,
    context_frames,
    noise_levels,
    cotangent,
):
    clip_count, half_frames, patch_local, breadth = block_input.shape
    patches_all = patch_local * lax.axis_size("tensor")
    head_cols = w_qkv.shape[2]
    heads_local = head_cols // HD
    softmax_scale = HD ** (-0.5)
    frame_first = lax.axis_index("seq") * half_frames
    frame_ids = frame_first + jnp.arange(half_frames, dtype=jnp.int32)
    condition = level_features(noise_levels, context_frames, frame_ids, breadth).astype(
        jnp.bfloat16
    )
    modulation = jnp.einsum(
        "cfd,de->cfe", condition, w_mod, preferred_element_type=jnp.float32
    ) + b_mod.astype(jnp.float32)
    shift_one, scale_one, gate_one, shift_two, scale_two, gate_two = jnp.split(
        modulation[:, :, None, :], 6, axis=-1
    )
    normed_one, inverse_one = normalize(block_input)
    attn_in = (normed_one * (1.0 + scale_one) + shift_one).astype(jnp.bfloat16)
    attn_all = lax.all_gather(attn_in, "tensor", axis=2, tiled=True)
    projected = jnp.einsum("cfpd,dke->cfpke", attn_all, w_qkv, preferred_element_type=jnp.float32)
    bias_float = qv_bias.astype(jnp.float32)
    queries = (projected[..., 0, :] + bias_float[0]).astype(jnp.bfloat16)
    key_local = projected[..., 1, :].astype(jnp.bfloat16)
    value_local = (projected[..., 2, :] + bias_float[1]).astype(jnp.bfloat16)
    key_clip, value_clip = (
        lax.all_gather(key_local, "seq", axis=1, tiled=True),
        lax.all_gather(value_local, "seq", axis=1, tiled=True),
    )
    query_rows = half_frames * patches_all
    block_rows = min(512, query_rows)
    block_count = query_rows // block_rows
    key_rows = key_clip.shape[1] * patches_all
    key_frame = jnp.arange(key_rows, dtype=jnp.int32) // patches_all
    query_frames = (frame_first + jnp.arange(query_rows, dtype=jnp.int32) // patches_all).reshape(
        block_count, block_rows
    )
    query_heads = queries.reshape(clip_count, block_count, block_rows, heads_local, HD)
    key_heads = key_clip.reshape(clip_count, key_rows, heads_local, HD)
    value_heads = value_clip.reshape(clip_count, key_rows, heads_local, HD)

    def masked_scores(query_block, keys, frames_block, context_limit):
        scores = (
            jnp.einsum("bhd,khd->hbk", query_block, keys, preferred_element_type=jnp.float32)
            * softmax_scale
        )
        allowed = (key_frame[None, :] <= frames_block[:, None]) | (
            key_frame[None, :] < context_limit
        )
        return jnp.where(allowed[None], scores, -1e30)

    def forward_clip(members):
        clip_queries, keys, values, context_limit = members

        def forward_block(slices):
            query_block, frames_block = slices
            scores = masked_scores(query_block, keys, frames_block, context_limit)
            row_max = jnp.max(scores, axis=-1, keepdims=True)
            exponent = jnp.exp(scores - row_max)
            denominator = jnp.sum(exponent, axis=-1, keepdims=True)
            probability = (exponent / denominator).astype(jnp.bfloat16)
            result = jnp.einsum(
                "hbk,khd->bhd", probability, values, preferred_element_type=jnp.float32
            )
            return (result.astype(jnp.bfloat16), (row_max + jnp.log(denominator))[..., 0])

        return lax.map(forward_block, (clip_queries, query_frames))

    attended, log_total = lax.map(
        forward_clip, (query_heads, key_heads, value_heads, context_frames)
    )
    attended_rows = attended.reshape(clip_count, half_frames, patches_all, head_cols)
    portion = attended_rows
    branch_rows = lax.psum_scatter(
        jnp.einsum("cfpe,ed->pcfd", portion, w_out, preferred_element_type=jnp.float32).astype(
            jnp.bfloat16
        ),
        "tensor",
        scatter_dimension=0,
        tiled=True,
    ).astype(jnp.float32)
    branch_one = jnp.transpose(branch_rows, (1, 2, 0, 3)) + b_out.astype(jnp.float32)
    hidden_one = block_input + gate_one * branch_one
    normed_two, inverse_two = normalize(hidden_one)
    mlp_in = (normed_two * (1.0 + scale_two) + shift_two).astype(jnp.bfloat16)
    mlp_all = lax.all_gather(mlp_in, "tensor", axis=2, tiled=True)
    pre_act = jnp.einsum(
        "cfpd,de->cfpe", mlp_all, w_up, preferred_element_type=jnp.float32
    ) + b_up.astype(jnp.float32)
    activated = jax.nn.gelu(pre_act, approximate=True).astype(jnp.bfloat16)
    portion = activated
    mlp_rows = lax.psum_scatter(
        jnp.einsum("cfpe,ed->pcfd", portion, w_down, preferred_element_type=jnp.float32).astype(
            jnp.bfloat16
        ),
        "tensor",
        scatter_dimension=0,
        tiled=True,
    ).astype(jnp.float32)
    mlp_out = jnp.transpose(mlp_rows, (1, 2, 0, 3)) + b_down.astype(jnp.float32)
    output = hidden_one + gate_two * mlp_out
    grad_mlp = gate_two * cotangent
    grad_gate_two = jnp.sum(cotangent * mlp_out, axis=2)
    grad_b_down = jnp.sum(grad_mlp, axis=(0, 1, 2))
    grad_mlp_low = grad_mlp.astype(jnp.bfloat16)
    grad_mlp_all = lax.all_gather(grad_mlp_low, "tensor", axis=2, tiled=True)
    grad_act = jnp.einsum("cfpd,ed->cfpe", grad_mlp_all, w_down, preferred_element_type=jnp.float32)
    grad_w_down = jnp.einsum(
        "cfpe,cfpd->ed", activated, grad_mlp_all, preferred_element_type=jnp.float32
    )
    grad_pre = gelu_back(pre_act, grad_act).astype(jnp.bfloat16)
    grad_b_up = jnp.sum(grad_pre.astype(jnp.float32), axis=(0, 1, 2))
    grad_w_up = jnp.einsum("cfpd,cfpe->de", mlp_all, grad_pre, preferred_element_type=jnp.float32)
    portion = grad_pre
    grad_mlp_rows = lax.psum_scatter(
        jnp.einsum("cfpe,de->pcfd", portion, w_up, preferred_element_type=jnp.float32).astype(
            jnp.bfloat16
        ),
        "tensor",
        scatter_dimension=0,
        tiled=True,
    ).astype(jnp.float32)
    grad_mlp_in = jnp.transpose(grad_mlp_rows, (1, 2, 0, 3))
    grad_shift_two = jnp.sum(grad_mlp_in, axis=2)
    grad_scale_two = jnp.sum(grad_mlp_in * normed_two, axis=2)
    grad_hidden = cotangent + norm_back(grad_mlp_in * (1.0 + scale_two), normed_two, inverse_two)
    grad_branch = gate_one * grad_hidden
    grad_gate_one = jnp.sum(grad_hidden * branch_one, axis=2)
    grad_b_out = jnp.sum(grad_branch, axis=(0, 1, 2))
    grad_branch_all = lax.all_gather(grad_branch.astype(jnp.bfloat16), "tensor", axis=2, tiled=True)
    grad_attended = jnp.einsum(
        "cfpd,ed->cfpe", grad_branch_all, w_out, preferred_element_type=jnp.float32
    ).astype(jnp.bfloat16)
    grad_w_out = jnp.einsum(
        "cfpe,cfpd->ed", attended_rows, grad_branch_all, preferred_element_type=jnp.float32
    )
    grad_heads = grad_attended.reshape(clip_count, block_count, block_rows, heads_local, HD)

    def backward_clip(members):
        clip_queries, keys, values, context_limit, clip_grads, clip_totals = members

        def backward_block(running, slices):
            key_acc, value_acc = running
            query_block, frames_block, grad_block, total_block = slices
            scores = masked_scores(query_block, keys, frames_block, context_limit)
            probability = jnp.exp(scores - total_block[..., None])
            grad_prob = jnp.einsum(
                "bhd,khd->hbk", grad_block, values, preferred_element_type=jnp.float32
            )
            inner_sum = jnp.sum(probability * grad_prob, axis=-1, keepdims=True)
            grad_scores = (probability * (grad_prob - inner_sum)).astype(jnp.bfloat16)
            grad_query = (
                jnp.einsum("hbk,khd->bhd", grad_scores, keys, preferred_element_type=jnp.float32)
                * softmax_scale
            )
            key_acc = (
                key_acc
                + jnp.einsum(
                    "hbk,bhd->khd", grad_scores, query_block, preferred_element_type=jnp.float32
                )
                * softmax_scale
            )
            value_acc = value_acc + jnp.einsum(
                "hbk,bhd->khd",
                probability.astype(jnp.bfloat16),
                grad_block,
                preferred_element_type=jnp.float32,
            )
            return ((key_acc, value_acc), grad_query.astype(jnp.bfloat16))

        empty_acc = jnp.zeros((key_rows, heads_local, HD), jnp.float32)
        (grad_keys, grad_values), grad_queries = lax.scan(
            backward_block,
            (empty_acc, empty_acc),
            (clip_queries, query_frames, clip_grads, clip_totals),
        )
        return (grad_queries, grad_keys, grad_values)

    grad_queries, grad_keys, grad_values = lax.map(
        backward_clip, (query_heads, key_heads, value_heads, context_frames, grad_heads, log_total)
    )
    key_shape = (clip_count, key_clip.shape[1], patches_all, head_cols)
    grad_key_own, grad_value_own = (
        lax.psum_scatter(
            grad_keys.reshape(key_shape).astype(jnp.bfloat16),
            "seq",
            scatter_dimension=1,
            tiled=True,
        ).astype(jnp.float32),
        lax.psum_scatter(
            grad_values.reshape(key_shape).astype(jnp.bfloat16),
            "seq",
            scatter_dimension=1,
            tiled=True,
        ).astype(jnp.float32),
    )
    grad_qkv = jnp.stack(
        [
            grad_queries.reshape(clip_count, half_frames, patches_all, head_cols),
            grad_key_own.astype(jnp.bfloat16),
            grad_value_own.astype(jnp.bfloat16),
        ],
        axis=3,
    )
    grad_w_qkv = jnp.einsum(
        "cfpd,cfpke->dke", attn_all, grad_qkv, preferred_element_type=jnp.float32
    )
    grad_qv_bias = jnp.sum(grad_qkv[:, :, :, 0::2, :].astype(jnp.float32), axis=(0, 1, 2))
    portion = grad_qkv
    grad_attn_rows = lax.psum_scatter(
        jnp.einsum("cfpke,dke->pcfd", portion, w_qkv, preferred_element_type=jnp.float32).astype(
            jnp.bfloat16
        ),
        "tensor",
        scatter_dimension=0,
        tiled=True,
    ).astype(jnp.float32)
    grad_attn_in = jnp.transpose(grad_attn_rows, (1, 2, 0, 3))
    grad_shift_one = jnp.sum(grad_attn_in, axis=2)
    grad_scale_one = jnp.sum(grad_attn_in * normed_one, axis=2)
    grad_input = grad_hidden + norm_back(grad_attn_in * (1.0 + scale_one), normed_one, inverse_one)
    grad_modulation = jnp.concatenate(
        [
            grad_shift_one,
            grad_scale_one,
            grad_gate_one,
            grad_shift_two,
            grad_scale_two,
            grad_gate_two,
        ],
        axis=-1,
    )
    grad_modulation = grad_modulation.reshape(clip_count * half_frames, 6 * breadth)
    modulation_cols, out_bias_part, down_bias_part = (
        lax.psum_scatter(
            grad_modulation.astype(jnp.bfloat16), "tensor", scatter_dimension=1, tiled=True
        ).astype(jnp.float32),
        lax.psum_scatter(
            grad_b_out.astype(jnp.bfloat16), "tensor", scatter_dimension=0, tiled=True
        ).astype(jnp.float32),
        lax.psum_scatter(
            grad_b_down.astype(jnp.bfloat16), "tensor", scatter_dimension=0, tiled=True
        ).astype(jnp.float32),
    )
    condition_rows = condition.reshape(clip_count * half_frames, breadth).astype(jnp.float32)
    grad_w_mod = jnp.dot(condition_rows.T, modulation_cols, precision=lax.Precision.HIGHEST)
    grad_b_mod = jnp.sum(modulation_cols, axis=0)
    (
        total_w_qkv,
        total_qv_bias,
        total_w_out,
        total_b_out,
        total_w_up,
        total_b_up,
        total_w_down,
        total_b_down,
        total_w_mod,
        total_b_mod,
    ) = (
        lax.psum(grad_w_qkv.astype(jnp.bfloat16), ("dp", "seq")).astype(jnp.float32),
        lax.psum(grad_qv_bias.astype(jnp.bfloat16), ("dp", "seq")).astype(jnp.float32),
        lax.psum(grad_w_out.astype(jnp.bfloat16), ("dp", "seq")).astype(jnp.float32),
        lax.psum(out_bias_part.astype(jnp.bfloat16), ("dp", "seq")).astype(jnp.float32),
        lax.psum(grad_w_up.astype(jnp.bfloat16), ("dp", "seq")).astype(jnp.float32),
        lax.psum(grad_b_up.astype(jnp.bfloat16), ("dp", "seq")).astype(jnp.float32),
        lax.psum(grad_w_down.astype(jnp.bfloat16), ("dp", "seq")).astype(jnp.float32),
        lax.psum(down_bias_part.astype(jnp.bfloat16), ("dp", "seq")).astype(jnp.float32),
        lax.psum(grad_w_mod.astype(jnp.bfloat16), ("dp", "seq")).astype(jnp.float32),
        lax.psum(grad_b_mod.astype(jnp.bfloat16), ("dp", "seq")).astype(jnp.float32),
    )
    return (
        output,
        grad_input,
        total_w_qkv,
        total_qv_bias,
        total_w_out,
        total_b_out,
        total_w_up,
        total_b_up,
        total_w_down,
        total_b_down,
        total_w_mod,
        total_b_mod,
    )


def solution(mesh):
    placed = (
        P("dp", "seq", "tensor", None),
        P(None, None, "tensor"),
        P(None, "tensor"),
        P("tensor", None),
        P(),
        P(None, "tensor"),
        P("tensor"),
        P("tensor", None),
        P(),
        P(),
        P(),
        P("dp"),
        P("dp", "seq"),
        P("dp", "seq", "tensor", None),
    )
    return jax.shard_map(
        body,
        mesh=mesh,
        in_specs=placed,
        out_specs=(
            P("dp", "seq", "tensor", None),
            P("dp", "seq", "tensor", None),
            P(None, None, "tensor"),
            P(None, "tensor"),
            P("tensor", None),
            P("tensor"),
            P(None, "tensor"),
            P("tensor"),
            P("tensor", None),
            P("tensor"),
            P(None, "tensor"),
            P("tensor"),
        ),
        check_vma=False,
    )
```

profile of v0, /device:TPU:0, one launch (start us, length us, event | category | flops | bytes accessed | tf_op | source)
XLA Modules:
  0.0 1632.9 jit_solution(15091767421687436867)
XLA Ops:
  21.3 83.5 %all-gather.8.cloned.1.call-done = bf16[1,8,256,1024]{3,2,1,0:T(8,128)(2,1)} async-done(((bf16[1,8,64,1024]{3,2,1,0:T(8,128)(2,1)}), bf16[1,8,256,1024]{3,2,1,0:T(8,128)(2,1)}) %all-gather.8.cloned.1.call-update) | async-done | bytes 4194320 | tf_op jit(solution)/shard_map/all_gather | solution.py:70
  147.6 198.6 %while.50 = (s32[]{:T(128)}, bf16[4,512,4,64]{1,3,2,0:T(8,128)(2,1)S(1)}, f32[4,4,512]{2,1,0:T(4,128)S(1)}, s32[4,512]{1,0:T(4,128)S(1)}, s32[]{:T(128)}, /*inde...) while((s32[]{:T(128)}, ...), condition=%wide.region_5.6_spmd.clone.clone, body=%wide.region_2.5_spmd.clone.clone.sunk | while | flops 2252539904 | bytes 122271888 | solution.py:117
  150.0 16.0 fusion.176
  166.1 15.0 fusion.177
  181.1 16.3 fusion.178
  199.6 16.0 fusion.176
  215.7 15.0 fusion.177
  230.7 16.3 fusion.178
  249.2 16.0 fusion.176
  265.3 15.0 fusion.177
  280.3 16.3 fusion.178
  298.8 16.0 fusion.176
  314.9 15.0 fusion.177
  329.9 16.3 fusion.178
  354.7 76.7 %reduce-scatter.8.cloned.1.call-done = bf16[64,1,8,1024]{3,0,2,1:T(8,128)(2,1)} async-done(((bf16[256,1,8,1024]{3,0,2,1:T(8,128)(2,1)}), bf16[64,1,8,1024]{3,0,2,1:T(8,128)(2,1)}) %reduce-scatter.8.cloned.1.call-update) | async-done | bytes 1048592 | tf_op jit(solution)/shard_map/reduce_scatter | solution.py:124
  436.6 81.3 %all-gather.12.cloned.1.call-done = bf16[1,8,256,1024]{3,2,1,0:T(8,128)(2,1)} async-done(((bf16[1,8,64,1024]{3,2,1,0:T(8,128)(2,1)}), bf16[1,8,256,1024]{3,2,1,0:T(8,128)(2,1)}) %all-gather.12.cloned.1.call-update) | async-done | bytes 4194320 | tf_op jit(solution)/shard_map/all_gather | solution.py:136
  535.7 74.8 %reduce-scatter.10.cloned.1.call-done = bf16[64,1,8,1024]{3,0,2,1:T(8,128)(2,1)} async-done(((bf16[256,1,8,1024]{3,0,2,1:T(8,128)(2,1)}), bf16[64,1,8,1024]{3,0,2,1:T(8,128)(2,1)}) %reduce-scatter.10.cloned.1.call-update) | async-done | bytes 1048592 | tf_op jit(solution)/shard_map/reduce_scatter | solution.py:142
  614.5 81.4 %all-gather.14.cloned.1.call-done = bf16[1,8,256,1024]{3,2,1,0:T(8,128)(2,1)} async-done(((bf16[1,8,64,1024]{3,2,1,0:T(8,128)(2,1)}), bf16[1,8,256,1024]{3,2,1,0:T(8,128)(2,1)}) %all-gather.14.cloned.1.call-update) | async-done | bytes 4194320 | tf_op jit(solution)/shard_map/all_gather | solution.py:156
  695.9 13.3 fusion.144
  717.5 75.4 %reduce-scatter.12.cloned.1.call-done = bf16[64,1,8,1024]{3,0,2,1:T(8,128)(2,1)} async-done(((bf16[256,1,8,1024]{3,0,2,1:T(8,128)(2,1)}), bf16[64,1,8,1024]{3,0,2,1:T(8,128)(2,1)}) %reduce-scatter.12.cloned.1.call-update) | async-done | bytes 1048592 | tf_op jit(solution)/shard_map/reduce_scatter | solution.py:165
  803.0 81.3 %all-gather.16.cloned.1.call-done = bf16[1,8,256,1024]{3,2,1,0:T(8,128)(2,1)} async-done(((bf16[1,8,64,1024]{3,2,1,0:T(8,128)(2,1)}), bf16[1,8,256,1024]{3,2,1,0:T(8,128)(2,1)}) %all-gather.16.cloned.1.call-update) | async-done | bytes 4194320 | tf_op jit(solution)/shard_map/all_gather | solution.py:180
  892.2 435.7 %while.51 = (s32[]{:T(128)}, f32[4096,4,64]{0,2,1:T(8,128)}, f32[4096,4,64]{0,2,1:T(8,128)}, bf16[4,512,4,64]{1,3,2,0:T(8,128)(2,1)}, bf16[4,512,4,64]{1,3,2,0:T...) while((s32[]{:T(128)}, f32[4096,4,64]{0,2,1:T(8,128)}, ...), condition=%wide.region_15.16_spmd.clone.clone, body=%wide.region_13.15_spmd.clone.clone.sunk | while | flops 5504305152 | bytes 351639744 | solution.py:222
  894.6 17.3 %fusion.188 = f32[4,512,4096]{2,1,0:T(8,128)} fusion(bf16[4096,4,64]{0,2,1:T(8,128)(2,1)} %get-tuple-element.645, bf16[4,512,4,64]{1,3,2,0:T(8,128)(2,1)} %get-tuple-element.642, s32[]{:T(128)S(6)} %copy.131), kind=kOutput, calls=%fused_computation.48.clone.1 | convolution fusion | flops 1073741824 | bytes 35913732 | tf_op jit(solution)/shard_map/while/body/eval_jaxpr/while/body/eval_jaxpr/bhd,khd->hbk/dot_general | solution.py:94
  911.9 16.5 %fusion.190 = f32[4096,4,64]{0,2,1:T(8,128)} fusion(f32[4,512,4096]{2,1,0:T(8,128)} %fusion.188, f32[4,512]{1,0:T(4,128)S(1)} %dynamic-slice_bitcast_fusion.2, pred[512,4096]{1,0:T(8,128)(4,1)S(1)} %compare_or_fusion.5, f32[4096,4,64]{0,2,1:T(8,128)} %get-tuple-element.627, pred[]{:T(512)S(6)} %compare.9, ...), kind=kOutput, calls=%fused_computation.39.clone.1 | convolution fusion | flops 1109393408 | bytes 44310532 | tf_op jit(solution)/shard_map/while/body/eval_jaxpr/while/body/eval_jaxpr/hbk,bhd->khd/dot_general | solution.py:213
  928.4 25.9 %multiply_reduce_fusion.6 = (f32[4,512]{1,0:T(4,128)S(1)}, f32[4,512,4096]{2,1,0:T(8,128)}) fusion(f32[4,512,4096]{2,1,0:T(8,128)} %fusion.188, f32[4,512]{1,0:T(4,128)S(1)} %dynamic-slice_bitcast_fusion.2, pred[512,4096]{1,0:T(8,128)(4,1)S(1)} %compare_or_fusion.5, bf16[4096,4,64]{0,2,1:T(8,128)(2,1)} %get-tuple-element.648, ...), kind=kOutput, calls=%fused_computation.29.clone.1 | convolution fusion | flops 1115682816 | bytes 71581696 | tf_op jit(solution)/shard_map/while/body/eval_jaxpr/while/body/eval_jaxpr/bhd,khd->hbk/dot_general | solution.py:197
  954.3 27.6 %multiply_convert_fusion.10 = bf16[4,512,4096]{2,1,0:T(8,128)(2,1)} fusion(f32[4,512,4096]{2,1,0:T(8,128)} %get-tuple-element.583, f32[4,512,4096]{2,1,0:T(8,128)} %fusion.188, f32[4,512]{1,0:T(4,128)S(1)} %get-tuple-element.584, f32[4,512]{1,0:T(4,128)S(1)} %dynamic-slice_bitcast_fusion.2, pred[512,4096]{1,0:T(8,128)(4,1)S(1)} %compare_or_fusion.5), kind=kLoop, calls=%fused_computation.28.clone.1 | loop fusion | flops 50331648 | bytes 85999616 | tf_op jit(solution)/shard_map/while/body/eval_jaxpr/while/body/eval_jaxpr/convert_element_type | solution.py:201
  981.9 10.1 fusion.191
  1001.5 17.3 %fusion.188 = f32[4,512,4096]{2,1,0:T(8,128)} fusion(bf16[4096,4,64]{0,2,1:T(8,128)(2,1)} %get-tuple-element.645, bf16[4,512,4,64]{1,3,2,0:T(8,128)(2,1)} %get-tuple-element.642, s32[]{:T(128)S(6)} %copy.131), kind=kOutput, calls=%fused_computation.48.clone.1 | convolution fusion | flops 1073741824 | bytes 35913732 | tf_op jit(solution)/shard_map/while/body/eval_jaxpr/while/body/eval_jaxpr/bhd,khd->hbk/dot_general | solution.py:94
  1018.8 17.7 %fusion.190 = f32[4096,4,64]{0,2,1:T(8,128)} fusion(f32[4,512,4096]{2,1,0:T(8,128)} %fusion.188, f32[4,512]{1,0:T(4,128)S(1)} %dynamic-slice_bitcast_fusion.2, pred[512,4096]{1,0:T(8,128)(4,1)S(1)} %compare_or_fusion.5, f32[4096,4,64]{0,2,1:T(8,128)} %get-tuple-element.627, pred[]{:T(512)S(6)} %compare.9, ...), kind=kOutput, calls=%fused_computation.39.clone.1 | convolution fusion | flops 1109393408 | bytes 44310532 | tf_op jit(solution)/shard_map/while/body/eval_jaxpr/while/body/eval_jaxpr/hbk,bhd->khd/dot_general | solution.py:213
  1036.5 25.9 %multiply_reduce_fusion.6 = (f32[4,512]{1,0:T(4,128)S(1)}, f32[4,512,4096]{2,1,0:T(8,128)}) fusion(f32[4,512,4096]{2,1,0:T(8,128)} %fusion.188, f32[4,512]{1,0:T(4,128)S(1)} %dynamic-slice_bitcast_fusion.2, pred[512,4096]{1,0:T(8,128)(4,1)S(1)} %compare_or_fusion.5, bf16[4096,4,64]{0,2,1:T(8,128)(2,1)} %get-tuple-element.648, ...), kind=kOutput, calls=%fused_computation.29.clone.1 | convolution fusion | flops 1115682816 | bytes 71581696 | tf_op jit(solution)/shard_map/while/body/eval_jaxpr/while/body/eval_jaxpr/bhd,khd->hbk/dot_general | solution.py:197
  1062.4 27.6 %multiply_convert_fusion.10 = bf16[4,512,4096]{2,1,0:T(8,128)(2,1)} fusion(f32[4,512,4096]{2,1,0:T(8,128)} %get-tuple-element.583, f32[4,512,4096]{2,1,0:T(8,128)} %fusion.188, f32[4,512]{1,0:T(4,128)S(1)} %get-tuple-element.584, f32[4,512]{1,0:T(4,128)S(1)} %dynamic-slice_bitcast_fusion.2, pred[512,4096]{1,0:T(8,128)(4,1)S(1)} %compare_or_fusion.5), kind=kLoop, calls=%fused_computation.28.clone.1 | loop fusion | flops 50331648 | bytes 85999616 | tf_op jit(solution)/shard_map/while/body/eval_jaxpr/while/body/eval_jaxpr/convert_element_type | solution.py:201
  1090.0 10.1 fusion.191
  1110.9 17.3 %fusion.188 = f32[4,512,4096]{2,1,0:T(8,128)} fusion(bf16[4096,4,64]{0,2,1:T(8,128)(2,1)} %get-tuple-element.645, bf16[4,512,4,64]{1,3,2,0:T(8,128)(2,1)} %get-tuple-element.642, s32[]{:T(128)S(6)} %copy.131), kind=kOutput, calls=%fused_computation.48.clone.1 | convolution fusion | flops 1073741824 | bytes 35913732 | tf_op jit(solution)/shard_map/while/body/eval_jaxpr/while/body/eval_jaxpr/bhd,khd->hbk/dot_general | solution.py:94
  1128.2 17.7 %fusion.190 = f32[4096,4,64]{0,2,1:T(8,128)} fusion(f32[4,512,4096]{2,1,0:T(8,128)} %fusion.188, f32[4,512]{1,0:T(4,128)S(1)} %dynamic-slice_bitcast_fusion.2, pred[512,4096]{1,0:T(8,128)(4,1)S(1)} %compare_or_fusion.5, f32[4096,4,64]{0,2,1:T(8,128)} %get-tuple-element.627, pred[]{:T(512)S(6)} %compare.9, ...), kind=kOutput, calls=%fused_computation.39.clone.1 | convolution fusion | flops 1109393408 | bytes 44310532 | tf_op jit(solution)/shard_map/while/body/eval_jaxpr/while/body/eval_jaxpr/hbk,bhd->khd/dot_general | solution.py:213
  1145.9 25.9 %multiply_reduce_fusion.6 = (f32[4,512]{1,0:T(4,128)S(1)}, f32[4,512,4096]{2,1,0:T(8,128)}) fusion(f32[4,512,4096]{2,1,0:T(8,128)} %fusion.188, f32[4,512]{1,0:T(4,128)S(1)} %dynamic-slice_bitcast_fusion.2, pred[512,4096]{1,0:T(8,128)(4,1)S(1)} %compare_or_fusion.5, bf16[4096,4,64]{0,2,1:T(8,128)(2,1)} %get-tuple-element.648, ...), kind=kOutput, calls=%fused_computation.29.clone.1 | convolution fusion | flops 1115682816 | bytes 71581696 | tf_op jit(solution)/shard_map/while/body/eval_jaxpr/while/body/eval_jaxpr/bhd,khd->hbk/dot_general | solution.py:197
  1171.8 27.6 %multiply_convert_fusion.10 = bf16[4,512,4096]{2,1,0:T(8,128)(2,1)} fusion(f32[4,512,4096]{2,1,0:T(8,128)} %get-tuple-element.583, f32[4,512,4096]{2,1,0:T(8,128)} %fusion.188, f32[4,512]{1,0:T(4,128)S(1)} %get-tuple-element.584, f32[4,512]{1,0:T(4,128)S(1)} %dynamic-slice_bitcast_fusion.2, pred[512,4096]{1,0:T(8,128)(4,1)S(1)} %compare_or_fusion.5), kind=kLoop, calls=%fused_computation.28.clone.1 | loop fusion | flops 50331648 | bytes 85999616 | tf_op jit(solution)/shard_map/while/body/eval_jaxpr/while/body/eval_jaxpr/convert_element_type | solution.py:201
  1199.4 10.1 fusion.191
  1220.3 17.3 %fusion.188 = f32[4,512,4096]{2,1,0:T(8,128)} fusion(bf16[4096,4,64]{0,2,1:T(8,128)(2,1)} %get-tuple-element.645, bf16[4,512,4,64]{1,3,2,0:T(8,128)(2,1)} %get-tuple-element.642, s32[]{:T(128)S(6)} %copy.131), kind=kOutput, calls=%fused_computation.48.clone.1 | convolution fusion | flops 1073741824 | bytes 35913732 | tf_op jit(solution)/shard_map/while/body/eval_jaxpr/while/body/eval_jaxpr/bhd,khd->hbk/dot_general | solution.py:94
  1237.6 17.7 %fusion.190 = f32[4096,4,64]{0,2,1:T(8,128)} fusion(f32[4,512,4096]{2,1,0:T(8,128)} %fusion.188, f32[4,512]{1,0:T(4,128)S(1)} %dynamic-slice_bitcast_fusion.2, pred[512,4096]{1,0:T(8,128)(4,1)S(1)} %compare_or_fusion.5, f32[4096,4,64]{0,2,1:T(8,128)} %get-tuple-element.627, pred[]{:T(512)S(6)} %compare.9, ...), kind=kOutput, calls=%fused_computation.39.clone.1 | convolution fusion | flops 1109393408 | bytes 44310532 | tf_op jit(solution)/shard_map/while/body/eval_jaxpr/while/body/eval_jaxpr/hbk,bhd->khd/dot_general | solution.py:213
  1255.3 25.9 %multiply_reduce_fusion.6 = (f32[4,512]{1,0:T(4,128)S(1)}, f32[4,512,4096]{2,1,0:T(8,128)}) fusion(f32[4,512,4096]{2,1,0:T(8,128)} %fusion.188, f32[4,512]{1,0:T(4,128)S(1)} %dynamic-slice_bitcast_fusion.2, pred[512,4096]{1,0:T(8,128)(4,1)S(1)} %compare_or_fusion.5, bf16[4096,4,64]{0,2,1:T(8,128)(2,1)} %get-tuple-element.648, ...), kind=kOutput, calls=%fused_computation.29.clone.1 | convolution fusion | flops 1115682816 | bytes 71581696 | tf_op jit(solution)/shard_map/while/body/eval_jaxpr/while/body/eval_jaxpr/bhd,khd->hbk/dot_general | solution.py:197
  1281.2 27.6 %multiply_convert_fusion.10 = bf16[4,512,4096]{2,1,0:T(8,128)(2,1)} fusion(f32[4,512,4096]{2,1,0:T(8,128)} %get-tuple-element.583, f32[4,512,4096]{2,1,0:T(8,128)} %fusion.188, f32[4,512]{1,0:T(4,128)S(1)} %get-tuple-element.584, f32[4,512]{1,0:T(4,128)S(1)} %dynamic-slice_bitcast_fusion.2, pred[512,4096]{1,0:T(8,128)(4,1)S(1)} %compare_or_fusion.5), kind=kLoop, calls=%fused_computation.28.clone.1 | loop fusion | flops 50331648 | bytes 85999616 | tf_op jit(solution)/shard_map/while/body/eval_jaxpr/while/body/eval_jaxpr/convert_element_type | solution.py:201
  1308.8 10.1 fusion.191
  1348.5 10.5 reduce-scatter.16.cloned.1.call-done
  1376.3 11.0 bitcast_convert_fusion.1
  1389.7 55.0 %reduce-scatter.18.cloned.1.call-done = bf16[64,1,8,1024]{3,0,2,1:T(8,128)(2,1)} async-done(((bf16[256,1,8,1024]{3,0,2,1:T(8,128)(2,1)}), bf16[64,1,8,1024]{3,0,2,1:T(8,128)(2,1)}) %reduce-scatter.18.cloned.1.call-update) | async-done | bytes 1048592 | tf_op jit(solution)/shard_map/reduce_scatter | solution.py:260
  1457.0 12.5 reduce-scatter.20.cloned.1.call-done
  1488.5 13.2 all-reduce.2
  1504.7 106.7 %all-reduce.7.cloned.1.call-done = (bf16[1024,3,256]{2,0,1:T(8,128)(2,1)}, bf16[256,1024]{1,0:T(8,128)(2,1)}, bf16[1024,1024]{1,0:T(8,128)(2,1)}, bf16[1024,1024]{1,0:T(8,128)(2,1)}, bf16[1024,1536]{1,0:T(8,128)(2,1)}) async-done(((bf16[1024,3,256]{2,0,1:T(8,128)(2,1)}, bf16[256,1024]{1,0:T(8,128)(2,1)}, bf16[1024,1024]{1,0:T(8,128)(2,1)}, bf16[1024,1024]{1,0:T(8,128)(2,1)}, bf16[1024,1536]{1,0:T(8,128)(2,1)}), ...) | async-done | bytes 9437200 | tf_op jit(solution)/shard_map/psum | solution.py:310
  (300 shorter events, 255.5 us)
Async XLA Ops:
  7.2 520.9 %copy-start = (bf16[1024,1024]{1,0:T(8,128)(2,1)S(1)}, bf16[1024,1024]{1,0:T(8,128)(2,1)}, u32[]{:S(2)}) copy-start(bf16[1024,1024]{1,0:T(8,128)(2,1)} %param.25) | copy-start | bytes 6291460
  7.2 97.7 %all-gather.8.cloned.1.call-start = ((), (), s32[]{:S(2)}) async-start(), calls=%async_computation.7 | async-start | bytes 5242880 | tf_op jit(solution)/shard_map/all_gather | solution.py:70
  9.8 9.3 copy-start.33
  12.0 7.7 copy-start.4
  21.3 108.8 %all-gather.10.cloned.1.call-start = ((), (), s32[]{:S(2)}) async-start(), calls=%async_computation.8 | async-start | bytes 3145728 | tf_op jit(solution)/shard_map/all_gather | solution.py:78
  114.4 24.4 %all-gather.18.cloned.1.call-start = ((), (), s32[]{:S(2)}) async-start(), calls=%async_computation.19 | async-start | bytes 3145728 | tf_op jit(solution)/shard_map/all_gather | solution.py:77
  117.2 314.2 %reduce-scatter.8.cloned.1.call-start = ((), (), s32[]{:S(2)}) async-start(), calls=%async_computation.9 | async-start | bytes 5242880 | tf_op jit(solution)/shard_map/reduce_scatter | solution.py:124
  150.0 16.0 copy-start.3
  199.6 16.0 copy-start.3
  249.2 16.0 copy-start.3
  298.8 16.0 copy-start.3
  349.8 81.6 %copy-start.23 = (f32[8,1024]{1,0:T(8,128)S(1)}, f32[8,1024]{1,0:T(8,128)}, u32[]{:S(2)}) copy-start(f32[8,1024]{1,0:T(8,128)} %get-tuple-element.454) | copy-start | bytes 98308
  354.6 80.4 %copy-start.24 = (f32[8,1024]{1,0:T(8,128)S(1)}, f32[8,1024]{1,0:T(8,128)}, u32[]{:S(2)}) copy-start(f32[8,1024]{1,0:T(8,128)} %get-tuple-element.451) | copy-start | bytes 98308
  354.6 80.4 %copy-start.32 = (f32[8,1024]{1,0:T(8,128)S(1)}, f32[8,1024]{1,0:T(8,128)}, u32[]{:S(2)}) copy-start(f32[8,1024]{1,0:T(8,128)} %get-tuple-element.450) | copy-start | bytes 98308
  354.6 163.3 %all-gather.12.cloned.1.call-start = ((), (), s32[]{:S(2)}) async-start(), calls=%async_computation.10 | async-start | bytes 5242880 | tf_op jit(solution)/shard_map/all_gather | solution.py:136
  436.5 174.0 %reduce-scatter.10.cloned.1.call-start = ((), (), s32[]{:S(2)}) async-start(), calls=%async_computation.11 | async-start | bytes 5242880 | tf_op jit(solution)/shard_map/reduce_scatter | solution.py:142
  436.6 259.3 %copy-start.45 = (f32[1024]{0:T(1024)}, f32[1024]{0:T(1024)S(1)}, u32[]{:S(2)}) copy-start(f32[1024]{0:T(1024)S(1)} %convert_element_type.268) | copy-start | bytes 12292
  535.0 75.5 %copy-start.26 = (f32[8,1024]{1,0:T(8,128)S(1)}, f32[8,1024]{1,0:T(8,128)}, u32[]{:S(2)}) copy-start(f32[8,1024]{1,0:T(8,128)} %get-tuple-element.449) | copy-start | bytes 98308
  535.1 160.8 %all-gather.14.cloned.1.call-start = ((), (), s32[]{:S(2)}) async-start(), calls=%async_computation.12 | async-start | bytes 5242880 | tf_op jit(solution)/shard_map/all_gather | solution.py:156
  614.4 178.5 %reduce-scatter.12.cloned.1.call-start = ((), (), s32[]{:S(2)}) async-start(), calls=%async_computation.13 | async-start | bytes 5242880 | tf_op jit(solution)/shard_map/reduce_scatter | solution.py:165
  695.8 15.4 copy-start.54
  717.4 75.5 %copy-start.7 = (f32[1,8,64,1024]{3,2,1,0:T(8,128)S(1)}, f32[1,8,64,1024]{3,2,1,0:T(8,128)}, u32[]{:S(2)}) copy-start(f32[1,8,64,1024]{3,2,1,0:T(8,128)} %copy-done.6) | copy-start | bytes 6291460
  717.4 78.4 %copy-start.17 = (bf16[64,1,8,1024]{3,0,2,1:T(8,128)(2,1)S(1)}, bf16[64,1,8,1024]{3,0,2,1:T(8,128)(2,1)}, u32[]{:S(2)}) copy-start(bf16[64,1,8,1024]{3,0,2,1:T(8,128)(2,1)} %reduce-scatter.8.cloned.1.call-done) | copy-start | bytes 3145732
  717.5 166.9 %all-gather.16.cloned.1.call-start = ((), (), s32[]{:S(2)}) async-start(), calls=%async_computation.14 | async-start | bytes 5242880 | tf_op jit(solution)/shard_map/all_gather | solution.py:180
  800.4 84.0 %copy-start.25 = (bf16[256,1024]{1,0:T(8,128)(2,1)S(1)}, bf16[256,1024]{1,0:T(8,128)(2,1)}, u32[]{:S(2)}) copy-start(bf16[256,1024]{1,0:T(8,128)(2,1)} %param.21) | copy-start | bytes 1572868
  803.0 545.5 %reduce-scatter.14.cloned.1.call-start = ((), (), s32[]{:S(2)}) async-start(), calls=%async_computation.15 | async-start | bytes 3145728 | tf_op jit(solution)/shard_map/reduce_scatter | solution.py:234
  981.9 11.2 copy-start.2
  1090.0 11.2 copy-start.2
  1199.4 11.2 copy-start.2
  1308.8 11.2 copy-start.2
  1336.7 22.3 %reduce-scatter.16.cloned.1.call-start = ((), (), s32[]{:S(2)}) async-start(), calls=%async_computation.16 | async-start | bytes 3145728 | tf_op jit(solution)/shard_map/reduce_scatter | solution.py:240
  1345.6 99.1 %reduce-scatter.18.cloned.1.call-start = ((), (), s32[]{:S(2)}) async-start(), calls=%async_computation.17 | async-start | bytes 5242880 | tf_op jit(solution)/shard_map/reduce_scatter | solution.py:260
  1366.6 9.7 copy-start.46
  1366.6 102.9 %reduce-scatter.20.cloned.1.call-start = ((), (), s32[]{:S(2)}) async-start(), calls=%async_computation.18 | async-start | bytes 122880 | tf_op jit(solution)/shard_map/reduce_scatter | solution.py:285
  1366.8 9.5 copy-start.52
  1376.3 11.1 copy-start.11
  1376.3 11.3 copy-start.16
  1376.3 11.3 copy-start.53
  1387.6 58.6 %copy-start.5 = (f32[1,8,64,1024]{3,2,1,0:T(8,128)S(1)}, f32[1,8,64,1024]{3,2,1,0:T(8,128)}, u32[]{:S(2)}) copy-start(f32[1,8,64,1024]{3,2,1,0:T(8,128)} %param.18) | copy-start | bytes 6291460
  1387.6 58.6 %copy-start.22 = (f32[8,1024]{1,0:T(8,128)S(1)}, f32[8,1024]{1,0:T(8,128)}, u32[]{:S(2)}) copy-start(f32[8,1024]{1,0:T(8,128)} %copy-done.21) | copy-start | bytes 98308
  1387.6 58.6 %copy-start.34 = (f32[8,64]{1,0:T(8,128)S(1)}, f32[8,64]{1,0:T(8,128)}, u32[]{:S(2)}) copy-start(f32[8,64]{1,0:T(8,128)} %copy-done.33) | copy-start | bytes 6148
  1387.6 58.6 %copy-start.37 = (f32[8,64]{1,0:T(8,128)S(1)}, f32[8,64]{1,0:T(8,128)}, u32[]{:S(2)}) copy-start(f32[8,64]{1,0:T(8,128)} %copy-done.36) | copy-start | bytes 6148
  1389.7 59.0 %copy-start.40 = (bf16[8,1024]{1,0:T(8,128)(2,1)S(1)}, bf16[8,1024]{1,0:T(8,128)(2,1)}, u32[]{:S(2)}) copy-start(bf16[8,1024]{1,0:T(8,128)(2,1)} %get-tuple-element.386) | copy-start | bytes 49156
  1389.7 59.0 %copy-start.39 = (bf16[8,1024]{1,0:T(8,128)(2,1)S(1)}, bf16[8,1024]{1,0:T(8,128)(2,1)}, u32[]{:S(2)}) copy-start(bf16[8,1024]{1,0:T(8,128)(2,1)} %get-tuple-element.380) | copy-start | bytes 49156
  1389.7 59.0 %copy-start.38 = (bf16[8,1024]{1,0:T(8,128)(2,1)S(1)}, bf16[8,1024]{1,0:T(8,128)(2,1)}, u32[]{:S(2)}) copy-start(bf16[8,1024]{1,0:T(8,128)(2,1)} %get-tuple-element.384) | copy-start | bytes 49156
  1449.5 20.0 %copy-start.28 = (f32[8,512]{1,0:T(8,128)S(1)}, f32[8,512]{1,0:T(8,128)}, u32[]{:S(2)}) copy-start(f32[8,512]{1,0:T(8,128)} %copy-done.27) | copy-start | bytes 49156
  1449.5 20.0 %copy-start.30 = (f32[8,512]{1,0:T(8,128)S(1)}, f32[8,512]{1,0:T(8,128)}, u32[]{:S(2)}) copy-start(f32[8,512]{1,0:T(8,128)} %copy-done.29) | copy-start | bytes 49156
  1449.5 161.9 %all-reduce.7.cloned.1.call-start = ((), (), s32[]{:S(2)}) async-start(), calls=%async_computation.20 | async-start | bytes 18874368 | tf_op jit(solution)/shard_map/psum | solution.py:310
  (30 other events, 94.2 us)
Sparse Core Ops, SparseCore 0:
  21.4 83.4 all-gather.7
  114.6 9.0 all-gather.9
  125.8 11.7 all-gather.17
  354.7 76.6 reduce-scatter.7
  436.6 81.2 all-gather.11
  535.2 75.2 reduce-scatter.9
  614.6 81.2 all-gather.13
  717.6 75.2 reduce-scatter.11
  803.1 81.2 all-gather.15
  1336.8 8.2 reduce-scatter.13
  1347.9 11.0 reduce-scatter.15
  1366.7 78.0 reduce-scatter.17
  1449.6 19.8 reduce-scatter.19
  1474.8 136.5 all-reduce.6
where the time goes:
time: 1640 us; the launch traced here: 1630 us
  waiting for transfers between devices  739 us (45%)
  matrix products  536 us (33%)
  other arithmetic  244 us (15%)
  local copies, waits for them, and re-layouts  73.1 us (4%)
  blocking collectives  22.1 us (1%)
  between operations  16.4 us (1%)
    dot_general x8, matrix products, masked_scores(): jnp.einsum('bhd,khd->hbk', query_block, keys, preferred_element_type=jnp....  133 us
    convert_element_type x4, other arithmetic, backward_block(): grad_scores = (probability * (grad_prob - inner_sum)).astype(jnp.bfloat16)  110 us
    psum x1, waiting for transfers between devices, body(): lax.psum(grad_w_qkv.astype(jnp.bfloat16), ('dp', 'seq')).astype(jnp.float32)  107 us
    dot_general x4, matrix products, backward_block(): jnp.einsum('bhd,khd->hbk', grad_block, values, preferred_element_type=jnp...  104 us
    all_gather x1, waiting for transfers between devices, body(): attn_all = lax.all_gather(attn_in, 'tensor', axis=2, tiled=True)  83.5 us
    all_gather x1, waiting for transfers between devices, body(): grad_mlp_all = lax.all_gather(grad_mlp_low, 'tensor', axis=2, tiled=True)  81.4 us
    all_gather x1, waiting for transfers between devices, body(): mlp_all = lax.all_gather(mlp_in, 'tensor', axis=2, tiled=True)  81.3 us
    all_gather x1, waiting for transfers between devices, body(): lax.all_gather(grad_branch.astype(jnp.bfloat16), 'tensor', axis=2, tiled=...  81.3 us
  transfers between devices with their start and end apart: 14, of which 11 were waited for; matrix products, arithmetic and copies ran while one was open for 5% of the time, Pallas kernels for 0%

commit v1 on v0

--- a/solution.py
+++ b/solution.py
@@ -1,11 +1,117 @@
+import functools
 import math
 
 import jax
 import jax.numpy as jnp
 from jax import lax
+from jax.experimental import pallas as pl
+from jax.experimental.pallas import tpu as pltpu
 from jax.sharding import PartitionSpec as P
 
 HD = 64
+F32 = jnp.float32
+BF = jnp.bfloat16
+NT=(((1,),(1,)),((),()))
+def split_heads(block, out_ref, rows, heads):
+    lane=lax.broadcasted_iota(jnp.int32, block.shape, 1)//HD
+    for h in range(heads):
+        out_ref[h*rows:(h+1)*rows,:]=jnp.where(lane==h, block, jnp.zeros_like(block))
+def fwd_kernel(rows, heads, frames, nvis_ref, q_ref, k_ref, v_ref, o_ref, p_ref, linv_ref, vt_ref, s_ref, b_ref, acc_ref):
+    c=pl.program_id(0); i=pl.program_id(1)
+    total=k_ref.shape[1]
+    cols=q_ref.shape[2]
+    @pl.when(i==0)
+    def _():
+        @pl.loop(0,total//rows)
+        def _(j):
+            at=pl.ds(pl.multiple_of(j*rows,rows),rows)
+            vt_ref[:,at]=v_ref[0,at,:].T
+    n=nvis_ref[c*frames+i]
+    split_heads(q_ref[0]*jnp.asarray(HD**-0.5,BF), b_ref, rows, heads)
+    wide=heads*rows
+    def scan_scores(j, top):
+        at=pl.ds(pl.multiple_of(j*rows,rows),rows)
+        s=lax.dot_general(k_ref[0,at,:], b_ref[...], NT, preferred_element_type=F32)
+        s_ref[at,:]=s
+        return jnp.maximum(top, jnp.max(s.reshape(rows//8,8,wide),axis=0))
+    top=lax.fori_loop(0,n,scan_scores,jnp.full((8,wide),-jnp.inf,F32))
+    top=jnp.max(top,axis=0,keepdims=True)
+    acc_ref[...]=jnp.zeros_like(acc_ref)
+    def gather_values(j, mass):
+        at=pl.ds(pl.multiple_of(j*rows,rows),rows)
+        p=jnp.exp(s_ref[at,:]-top)
+        low=p.astype(BF)
+        p_ref[0,0,at,:]=low
+        for h in range(heads):
+            acc_ref[h*HD:(h+1)*HD,:]+=jnp.dot(vt_ref[h*HD:(h+1)*HD,at], low[:,h*rows:(h+1)*rows], preferred_element_type=F32)
+        return mass+jnp.sum(p.reshape(rows//8,8,wide),axis=0)
+    mass=lax.fori_loop(0,n,gather_values,jnp.zeros((8,wide),F32))
+    inv=1.0/jnp.sum(mass,axis=0,keepdims=True)
+    full=jnp.concatenate([jnp.broadcast_to(inv[:,h*rows:(h+1)*rows],(HD,rows)) for h in range(heads)],axis=0)
+    o_ref[0]=(acc_ref[...]*full).T.astype(BF)
+    linv_ref[0]=full.T
+def attn_fwd(nvis,q,k,v,rows):
+    C,Q,cols=q.shape; heads=cols//HD; frames=Q//rows; K=k.shape[1]
+    wide=heads*rows
+    qspec=pl.BlockSpec((1,rows,cols),lambda c,i,n:(c,i,0))
+    kspec=pl.BlockSpec((1,K,cols),lambda c,i,n:(c,0,0))
+    return pl.pallas_call(functools.partial(fwd_kernel,rows,heads,frames),
+      grid_spec=pltpu.PrefetchScalarGridSpec(num_scalar_prefetch=1,grid=(C,frames),
+        in_specs=[qspec,kspec,kspec],
+        out_specs=[qspec,pl.BlockSpec((1,1,K,wide),lambda c,i,n:(c,i,0,0)),qspec],
+        scratch_shapes=[pltpu.VMEM((cols,K),BF),pltpu.VMEM((K,wide),F32),pltpu.VMEM((wide,cols),BF),pltpu.VMEM((cols,rows),F32)]),
+      out_shape=[jax.ShapeDtypeStruct(q.shape,BF),jax.ShapeDtypeStruct((C,frames,K,wide),BF),jax.ShapeDtypeStruct(q.shape,F32)],
+      compiler_params=pltpu.CompilerParams(vmem_limit_bytes=60<<20),
+      name="attend_forward")(nvis,q,k,v)
+def bwd_kernel(rows, heads, frames, nvis_ref, q_ref, k_ref, v_ref, o_ref, do_ref, linv_ref, p_ref, dq_ref, dk_ref, dv_ref, kt_ref, bq_ref, bd_ref, dka_ref, dva_ref, dqt_ref):
+    c=pl.program_id(0); i=pl.program_id(1)
+    total=k_ref.shape[1]
+    @pl.when(i==0)
+    def _():
+        @pl.loop(0,total//rows)
+        def _(j):
+            at=pl.ds(pl.multiple_of(j*rows,rows),rows)
+            kt_ref[:,at]=k_ref[0,at,:].T
+            dka_ref[at,:]=jnp.zeros((rows,dka_ref.shape[1]),F32)
+            dva_ref[at,:]=jnp.zeros((rows,dka_ref.shape[1]),F32)
+    n=nvis_ref[c*frames+i]
+    split_heads(q_ref[0]*jnp.asarray(HD**-0.5,BF), bq_ref, rows, heads)
+    scaled=do_ref[0].astype(F32)*linv_ref[0]
+    split_heads(scaled.astype(BF), bd_ref, rows, heads)
+    prod=(scaled*o_ref[0].astype(F32)).T
+    delta=jnp.concatenate([jnp.sum(prod[h*HD:(h+1)*HD],axis=0,keepdims=True) for h in range(heads)],axis=1)
+    dqt_ref[...]=jnp.zeros_like(dqt_ref)
+    @pl.loop(0,n)
+    def _(j):
+        at=pl.ds(pl.multiple_of(j*rows,rows),rows)
+        dp=lax.dot_general(v_ref[0,at,:], bd_ref[...], NT, preferred_element_type=F32)
+        low=p_ref[0,0,at,:]
+        ds=(low.astype(F32)*(dp-delta)).astype(BF)
+        dva_ref[at,:]+=jnp.dot(low,bd_ref[...],preferred_element_type=F32)
+        dka_ref[at,:]+=jnp.dot(ds,bq_ref[...],preferred_element_type=F32)
+        for h in range(heads):
+            dqt_ref[h*HD:(h+1)*HD,:]+=jnp.dot(kt_ref[h*HD:(h+1)*HD,at], ds[:,h*rows:(h+1)*rows], preferred_element_type=F32)
+    dq_ref[0]=(dqt_ref[...].T*HD**-0.5).astype(BF)
+    @pl.when(i==frames-1)
+    def _():
+        @pl.loop(0,total//rows)
+        def _(j):
+            at=pl.ds(pl.multiple_of(j*rows,rows),rows)
+            dk_ref[0,at,:]=dka_ref[at,:].astype(BF)
+            dv_ref[0,at,:]=dva_ref[at,:].astype(BF)
+def attn_bwd(nvis,q,k,v,o,do,linv,p,rows):
+    C,Q,cols=q.shape; heads=cols//HD; frames=Q//rows; K=k.shape[1]
+    wide=heads*rows
+    qspec=pl.BlockSpec((1,rows,cols),lambda c,i,n:(c,i,0))
+    kspec=pl.BlockSpec((1,K,cols),lambda c,i,n:(c,0,0))
+    return pl.pallas_call(functools.partial(bwd_kernel,rows,heads,frames),
+      grid_spec=pltpu.PrefetchScalarGridSpec(num_scalar_prefetch=1,grid=(C,frames),
+        in_specs=[qspec,kspec,kspec,qspec,qspec,qspec,pl.BlockSpec((1,1,K,wide),lambda c,i,n:(c,i,0,0))],
+        out_specs=[qspec,kspec,kspec],
+        scratch_shapes=[pltpu.VMEM((cols,K),BF),pltpu.VMEM((wide,cols),BF),pltpu.VMEM((wide,cols),BF),pltpu.VMEM((K,cols),F32),pltpu.VMEM((K,cols),F32),pltpu.VMEM((cols,rows),F32)]),
+      out_shape=[jax.ShapeDtypeStruct(q.shape,BF),jax.ShapeDtypeStruct(k.shape,BF),jax.ShapeDtypeStruct(k.shape,BF)],
+      compiler_params=pltpu.CompilerParams(vmem_limit_bytes=60<<20),
+      name="attend_backward")(nvis,q,k,v,o,do,linv,p)
 
 
 def level_features(levels, context, frame_ids, breadth):
@@ -52,8 +158,6 @@
     clip_count, half_frames, patch_local, breadth = block_input.shape
     patches_all = patch_local * lax.axis_size("tensor")
     head_cols = w_qkv.shape[2]
-    heads_local = head_cols // HD
-    softmax_scale = HD ** (-0.5)
     frame_first = lax.axis_index("seq") * half_frames
     frame_ids = frame_first + jnp.arange(half_frames, dtype=jnp.int32)
     condition = level_features(noise_levels, context_frames, frame_ids, breadth).astype(
@@ -78,46 +182,13 @@
         lax.all_gather(value_local, "seq", axis=1, tiled=True),
     )
     query_rows = half_frames * patches_all
-    block_rows = min(512, query_rows)
-    block_count = query_rows // block_rows
     key_rows = key_clip.shape[1] * patches_all
-    key_frame = jnp.arange(key_rows, dtype=jnp.int32) // patches_all
-    query_frames = (frame_first + jnp.arange(query_rows, dtype=jnp.int32) // patches_all).reshape(
-        block_count, block_rows
-    )
-    query_heads = queries.reshape(clip_count, block_count, block_rows, heads_local, HD)
-    key_heads = key_clip.reshape(clip_count, key_rows, heads_local, HD)
-    value_heads = value_clip.reshape(clip_count, key_rows, heads_local, HD)
-
-    def masked_scores(query_block, keys, frames_block, context_limit):
-        scores = (
-            jnp.einsum("bhd,khd->hbk", query_block, keys, preferred_element_type=jnp.float32)
-            * softmax_scale
-        )
-        allowed = (key_frame[None, :] <= frames_block[:, None]) | (
-            key_frame[None, :] < context_limit
-        )
-        return jnp.where(allowed[None], scores, -1e30)
-
-    def forward_clip(members):
-        clip_queries, keys, values, context_limit = members
-
-        def forward_block(slices):
-            query_block, frames_block = slices
-            scores = masked_scores(query_block, keys, frames_block, context_limit)
-            row_max = jnp.max(scores, axis=-1, keepdims=True)
-            exponent = jnp.exp(scores - row_max)
-            denominator = jnp.sum(exponent, axis=-1, keepdims=True)
-            probability = (exponent / denominator).astype(jnp.bfloat16)
-            result = jnp.einsum(
-                "hbk,khd->bhd", probability, values, preferred_element_type=jnp.float32
-            )
-            return (result.astype(jnp.bfloat16), (row_max + jnp.log(denominator))[..., 0])
-
-        return lax.map(forward_block, (clip_queries, query_frames))
-
-    attended, log_total = lax.map(
-        forward_clip, (query_heads, key_heads, value_heads, context_frames)
+    visible = jnp.maximum(frame_ids[None, :] + 1, context_frames[:, None]).astype(jnp.int32).reshape(-1)
+    query_flat = queries.reshape(clip_count, query_rows, head_cols)
+    key_flat = key_clip.reshape(clip_count, key_rows, head_cols)
+    value_flat = value_clip.reshape(clip_count, key_rows, head_cols)
+    attended, weights_low, inverse_mass = attn_fwd(
+        visible, query_flat, key_flat, value_flat, patches_all
     )
     attended_rows = attended.reshape(clip_count, half_frames, patches_all, head_cols)
     portion = attended_rows
@@ -184,50 +255,16 @@
     grad_w_out = jnp.einsum(
         "cfpe,cfpd->ed", attended_rows, grad_branch_all, preferred_element_type=jnp.float32
     )
-    grad_heads = grad_attended.reshape(clip_count, block_count, block_rows, heads_local, HD)
-
-    def backward_clip(members):
-        clip_queries, keys, values, context_limit, clip_grads, clip_totals = members
-
-        def backward_block(running, slices):
-            key_acc, value_acc = running
-            query_block, frames_block, grad_block, total_block = slices
-            scores = masked_scores(query_block, keys, frames_block, context_limit)
-            probability = jnp.exp(scores - total_block[..., None])
-            grad_prob = jnp.einsum(
-                "bhd,khd->hbk", grad_block, values, preferred_element_type=jnp.float32
-            )
-            inner_sum = jnp.sum(probability * grad_prob, axis=-1, keepdims=True)
-            grad_scores = (probability * (grad_prob - inner_sum)).astype(jnp.bfloat16)
-            grad_query = (
-                jnp.einsum("hbk,khd->bhd", grad_scores, keys, preferred_element_type=jnp.float32)
-                * softmax_scale
-            )
-            key_acc = (
-                key_acc
-                + jnp.einsum(
-                    "hbk,bhd->khd", grad_scores, query_block, preferred_element_type=jnp.float32
-                )
-                * softmax_scale
-            )
-            value_acc = value_acc + jnp.einsum(
-                "hbk,bhd->khd",
-                probability.astype(jnp.bfloat16),
-                grad_block,
-                preferred_element_type=jnp.float32,
-            )
-            return ((key_acc, value_acc), grad_query.astype(jnp.bfloat16))
-
-        empty_acc = jnp.zeros((key_rows, heads_local, HD), jnp.float32)
-        (grad_keys, grad_values), grad_queries = lax.scan(
-            backward_block,
-            (empty_acc, empty_acc),
-            (clip_queries, query_frames, clip_grads, clip_totals),
-        )
-        return (grad_queries, grad_keys, grad_values)
-
-    grad_queries, grad_keys, grad_values = lax.map(
-        backward_clip, (query_heads, key_heads, value_heads, context_frames, grad_heads, log_total)
+    grad_queries, grad_keys, grad_values = attn_bwd(
+        visible,
+        query_flat,
+        key_flat,
+        value_flat,
+        attended,
+        grad_attended.reshape(clip_count, query_rows, head_cols),
+        inverse_mass,
+        weights_low,
+        patches_all,
     )
     key_shape = (clip_count, key_clip.shape[1], patches_all, head_cols)
     grad_key_own, grad_value_own = (

time: 1640 us -> 1160 us (0.71)
  matrix products: 536 us -> 95.1 us
  other arithmetic: 244 us -> 49.1 us
  Pallas kernels: 0 us -> 179 us
  local copies, waits for them, and re-layouts: 73.1 us -> 18 us
  waiting for transfers between devices: 739 us -> 756 us
    dot_general x28 -> x0, matrix products: 441 us -> none  [the longest x8 133 us: masked_scores(): jnp.einsum('bhd,khd->hbk', query_block, keys, preferred_element_type=jnp....]
    pallas_call x0 -> x2, Pallas kernels: none -> 179 us  [the longest x1 91.5 us: attn_bwd(): pl.pallas_call(functools.partial(bwd_kernel, rows, heads, frames), grid_s...]
    convert_element_type x7 -> x0, other arithmetic: 115 us -> none  [the longest x4 110 us: backward_block(): grad_scores = (probability * (grad_prob - inner_sum)).astype(jnp.bfloat16)]
    reduce_sum x4 -> x0, other arithmetic: 60.2 us -> none  [forward_block(): denominator = jnp.sum(exponent, axis=-1, keepdims=True)]
  transfers between devices with their start and end apart: 14 -> 14, of which waited for: 11 -> 14; matrix products, arithmetic and copies ran while one was open for 5% -> 4% of each run, Pallas kernels for 0% -> 0%
where the time goes in v1:
time: 1160 us; the launch traced here: 1150 us
  waiting for transfers between devices  756 us (65%)
  Pallas kernels  179 us (15%)
  matrix products  95.1 us (8%)
  other arithmetic  49.1 us (4%)
  blocking collectives  22.1 us (2%)
  local copies, waits for them, and re-layouts  18 us (2%)
  between operations  16.1 us (1%)
  starting transfers between devices  13.1 us (1%)
    psum x1, waiting for transfers between devices, body(): lax.psum(grad_w_qkv.astype(jnp.bfloat16), ('dp', 'seq')).astype(jnp.float32)  107 us
    pallas_call x1, Pallas kernels, attn_bwd(): pl.pallas_call(functools.partial(bwd_kernel, rows, heads, frames), grid_s...  91.5 us
    pallas_call x1, Pallas kernels, attn_fwd(): pl.pallas_call(functools.partial(fwd_kernel, rows, heads, frames), grid_s...  87.9 us
    all_gather x1, waiting for transfers between devices, body(): attn_all = lax.all_gather(attn_in, 'tensor', axis=2, tiled=True)  83.5 us
    all_gather x1, waiting for transfers between devices, body(): grad_mlp_all = lax.all_gather(grad_mlp_low, 'tensor', axis=2, tiled=True)  81.3 us
    all_gather x1, waiting for transfers between devices, body(): mlp_all = lax.all_gather(mlp_in, 'tensor', axis=2, tiled=True)  81 us
    reduce_scatter x1, waiting for transfers between devices, body(): lax.psum_scatter(jnp.einsum('cfpe,ed->pcfd', portion, w_out, preferred_el...  77.1 us
    reduce_scatter x1, waiting for transfers between devices, body(): lax.psum_scatter(jnp.einsum('cfpe,de->pcfd', portion, w_up, preferred_ele...  75.4 us
  transfers between devices with their start and end apart: 14, of which 14 were waited for; matrix products, arithmetic and copies ran while one was open for 4% of the time, Pallas kernels for 0%

profile of v1, /device:TPU:0, one launch (start us, length us, event | category | flops | bytes accessed | tf_op | source)
XLA Modules:
  0.0 1149.0 jit_solution(8773602714028123194)
XLA Ops:
  12.0 6.5 fusion.7
  20.1 83.5 %all-gather.8.cloned.1.call-done = bf16[1,8,256,1024]{3,2,1,0:T(8,128)(2,1)} async-done(((bf16[1,8,64,1024]{3,2,1,0:T(8,128)(2,1)}), bf16[1,8,256,1024]{3,2,1,0:T(8,128)(2,1)}) %all-gather.8.cloned.1.call-update) | async-done | bytes 4194320 | tf_op jit(solution)/shard_map/all_gather | solution.py:174
  103.6 5.7 fusion.26
  109.3 2.7 copy-done.10
  113.2 2.7 fusion.75
  118.7 3.6 all-gather.10.cloned.1.call-done
  122.4 13.9 %all-gather.18.cloned.1.call-done = bf16[1,16,256,1,256]{4,2,3,0,1:T(8,128)(2,1)} async-done(((bf16[1,8,256,1,256]{4,2,3,0,1:T(8,128)(2,1)}), bf16[1,16,256,1,256]{4,2,3,0,1:T(8,128)(2,1)}) %all-gather.18.cloned.1.call-update) | async-done | bytes 2097168 | tf_op jit(solution)/shard_map/all_gather | solution.py:181
  136.3 87.9 %attend_forward.1 = (bf16[1,2048,256]{2,1,0:T(8,128)(2,1)}, bf16[1,8,4096,1024]{3,2,1,0:T(8,128)(2,1)}, f32[1,2048,256]{2,1,0:T(8,128)}) custom-call(s32[8]{0:T(128)} %add_maximum_fusion.nvis_ref, bf16[1,2048,256]{2,1,0:T(8,128)(2,1)} %fusion.55.q_ref, bf16[1,4096,256]{2,1,0:T(8,128)(2,1)} %bitcast.214, bf16[1,4096,256]{2,1,0:T(8,128)(2,1)} %bitcast.212), custom_call_target="tpu_custom_call" | custom-call | tf_op jit(solution)/shard_map/attend_forward/pallas_call | solution.py:58
  224.2 4.5 convert_bitcast_fusion.2
  229.4 77.1 %reduce-scatter.8.cloned.1.call-done = bf16[64,1,8,1024]{3,0,2,1:T(8,128)(2,1)} async-done(((bf16[256,1,8,1024]{3,0,2,1:T(8,128)(2,1)}), bf16[64,1,8,1024]{3,0,2,1:T(8,128)(2,1)}) %reduce-scatter.8.cloned.1.call-update) | async-done | bytes 1048592 | tf_op jit(solution)/shard_map/reduce_scatter | solution.py:195
  306.6 2.3 fusion.84
  312.1 81.0 %all-gather.12.cloned.1.call-done = bf16[1,8,256,1024]{3,2,1,0:T(8,128)(2,1)} async-done(((bf16[1,8,64,1024]{3,2,1,0:T(8,128)(2,1)}), bf16[1,8,256,1024]{3,2,1,0:T(8,128)(2,1)}) %all-gather.12.cloned.1.call-update) | async-done | bytes 4194320 | tf_op jit(solution)/shard_map/all_gather | solution.py:207
  393.0 6.9 fusion.22
  400.0 3.2 copy-done.38
  403.2 7.0 convert_bitcast_fusion.1
  410.8 74.8 %reduce-scatter.10.cloned.1.call-done = bf16[64,1,8,1024]{3,0,2,1:T(8,128)(2,1)} async-done(((bf16[256,1,8,1024]{3,0,2,1:T(8,128)(2,1)}), bf16[64,1,8,1024]{3,0,2,1:T(8,128)(2,1)}) %reduce-scatter.10.cloned.1.call-update) | async-done | bytes 1048592 | tf_op jit(solution)/shard_map/reduce_scatter | solution.py:213
  485.6 3.9 fusion.48
  489.6 81.3 %all-gather.14.cloned.1.call-done = bf16[1,8,256,1024]{3,2,1,0:T(8,128)(2,1)} async-done(((bf16[1,8,64,1024]{3,2,1,0:T(8,128)(2,1)}), bf16[1,8,256,1024]{3,2,1,0:T(8,128)(2,1)}) %all-gather.14.cloned.1.call-update) | async-done | bytes 4194320 | tf_op jit(solution)/shard_map/all_gather | solution.py:227
  570.9 12.8 %fusion.87 = (bf16[1024]{0:T(1024)(128)(2,1)S(1)}, bf16[8,256,1024]{2,1,0:T(8,128)(2,1)S(1)}) fusion(f32[8,256,1024]{2,1,0:T(8,128)} %copy-done.38, f32[1024]{0:T(1024)S(1)} %convert_element_type.225, bf16[1024,1024]{1,0:T(8,128)(2,1)S(1)} %copy-done, bf16[1,8,256,1024]{3,2,1,0:T(8,128)(2,1)} %all-gather.14.cloned.1.call-done), kind=kOutput, calls=%fused_computation.135 | convolution fusion | flops 4341103616 | bytes 18880512 | tf_op jit(solution)/shard_map/cfpd,ed->cfpe/dot_general | solution.py:228
  585.7 6.2 convert_bitcast_fusion
  592.0 75.4 %reduce-scatter.12.cloned.1.call-done = bf16[64,1,8,1024]{3,0,2,1:T(8,128)(2,1)} async-done(((bf16[256,1,8,1024]{3,0,2,1:T(8,128)(2,1)}), bf16[64,1,8,1024]{3,0,2,1:T(8,128)(2,1)}) %reduce-scatter.12.cloned.1.call-update) | async-done | bytes 1048592 | tf_op jit(solution)/shard_map/reduce_scatter | solution.py:236
  667.4 2.4 fusion.39
  669.8 3.9 fusion.54
  676.3 12.2 %reduce-scatter.14.cloned.1.call-start = ((), (), s32[]{:S(2)}) async-start(), calls=%async_computation.15 | async-start | bytes 3145728 | tf_op jit(solution)/shard_map/reduce_scatter | solution.py:271
  688.5 69.2 %all-gather.16.cloned.1.call-done = bf16[1,8,256,1024]{3,2,1,0:T(8,128)(2,1)} async-done(((bf16[1,8,64,1024]{3,2,1,0:T(8,128)(2,1)}), bf16[1,8,256,1024]{3,2,1,0:T(8,128)(2,1)}) %all-gather.16.cloned.1.call-update) | async-done | bytes 4194320 | tf_op jit(solution)/shard_map/all_gather | solution.py:251
  757.7 4.5 fusion.66
  762.2 91.5 %attend_backward.1 = (bf16[1,2048,256]{2,1,0:T(8,128)(2,1)}, bf16[1,4096,256]{2,1,0:T(8,128)(2,1)}, bf16[1,4096,256]{2,1,0:T(8,128)(2,1)}) custom-call(s32[8]{0:T(128)} %add_maximum_fusion.nvis_ref, bf16[1,2048,256]{2,1,0:T(8,128)(2,1)} %fusion.55.q_ref, bf16[1,4096,256]{2,1,0:T(8,128)(2,1)} %bitcast.215, bf16[1,4096,256]{2,1,0:T(8,128)(2,1)} %bitcast.213, ...), custom_call_target="tpu_custom_call" | custom-call | tf_op jit(solution)/shard_map/attend_backward/pallas_call | solution.py:107
  854.5 6.9 reduce-scatter.14.cloned.1.call-done
  861.4 13.9 %reduce-scatter.16.cloned.1.call-done = bf16[1,8,256,256]{3,2,1,0:T(8,128)(2,1)} async-done(((bf16[1,16,256,256]{3,2,1,0:T(8,128)(2,1)}), bf16[1,8,256,256]{3,2,1,0:T(8,128)(2,1)}) %reduce-scatter.16.cloned.1.call-update) | async-done | bytes 1048592 | tf_op jit(solution)/shard_map/reduce_scatter | solution.py:277
  875.3 7.5 fusion.8
  882.9 9.5 bitcast_convert_fusion.2
  892.4 11.0 bitcast_convert_fusion.1
  903.7 2.1 fusion.72
  905.8 55.2 %reduce-scatter.18.cloned.1.call-done = bf16[64,1,8,1024]{3,0,2,1:T(8,128)(2,1)} async-done(((bf16[256,1,8,1024]{3,0,2,1:T(8,128)(2,1)}), bf16[64,1,8,1024]{3,0,2,1:T(8,128)(2,1)}) %reduce-scatter.18.cloned.1.call-update) | async-done | bytes 1048592 | tf_op jit(solution)/shard_map/reduce_scatter | solution.py:297
  962.5 2.4 fusion.44
  965.7 7.5 bitcast_convert_fusion.3
  973.1 12.5 %reduce-scatter.20.cloned.1.call-done = bf16[8,1536]{1,0:T(8,128)(2,1)} async-done(((bf16[8,6144]{1,0:T(8,128)(2,1)}), bf16[8,1536]{1,0:T(8,128)(2,1)}) %reduce-scatter.20.cloned.1.call-update) | async-done | bytes 24592 | tf_op jit(solution)/shard_map/reduce_scatter | solution.py:322
  985.7 3.4 convolution_convert_fusion
  991.0 8.9 all-reduce.4
  1000.0 2.0 pad_maximum_fusion
  1002.6 2.0 fusion.42
  1004.7 13.2 %all-reduce.2 = (bf16[2,256]{1,0:T(2,128)(2,1)S(1)}, bf16[256]{0:T(256)(128)(2,1)S(1)}, bf16[1024]{0:T(1024)(128)(2,1)S(1)}, bf16[256]{0:T(256)(128)(2,1)S(1)}, bf16[1536]{0:T(1024)(128)(2,1)S(1)}) all-reduce(bf16[2,256]{1,0:T(2,128)(2,1)S(1)} %slice_reduce_fusion, ...), channel_id=1, replica_groups=mesh['dp'=4,'seq'=2,'tensor'=4] {'dp','seq'}, use_global_device_ids=true, to_apply=%region_16.17 | all-reduce | flops 3584 | bytes 14336 | tf_op jit(solution)/shard_map/psum | solution.py:348
  1020.8 106.7 %all-reduce.7.cloned.1.call-done = (bf16[1024,3,256]{2,0,1:T(8,128)(2,1)}, bf16[256,1024]{1,0:T(8,128)(2,1)}, bf16[1024,1024]{1,0:T(8,128)(2,1)}, bf16[1024,1024]{1,0:T(8,128)(2,1)}, bf16[1024,1536]{1,0:T(8,128)(2,1)}) async-done(((bf16[1024,3,256]{2,0,1:T(8,128)(2,1)}, bf16[256,1024]{1,0:T(8,128)(2,1)}, bf16[1024,1024]{1,0:T(8,128)(2,1)}, bf16[1024,1024]{1,0:T(8,128)(2,1)}, bf16[1024,1536]{1,0:T(8,128)(2,1)}), ...) | async-done | bytes 9437200 | tf_op jit(solution)/shard_map/psum | solution.py:347
  1127.6 2.3 convert_element_type.249
  1129.8 3.3 convert_element_type.246
  1133.2 2.5 convert_element_type.253
  1135.7 2.5 convert_element_type.256
  1138.7 3.6 convert_element_type.261
  (148 shorter events, 27.4 us)
Async XLA Ops:
  7.2 396.0 %copy-start = (bf16[1024,1024]{1,0:T(8,128)(2,1)S(1)}, bf16[1024,1024]{1,0:T(8,128)(2,1)}, u32[]{:S(2)}) copy-start(bf16[1024,1024]{1,0:T(8,128)(2,1)} %param.21) | copy-start | bytes 6291460
  7.2 4.6 copy-start.26
  7.2 4.6 copy-start.32
  7.2 96.4 %all-gather.8.cloned.1.call-start = ((), (), s32[]{:S(2)}) async-start(), calls=%async_computation.7 | async-start | bytes 5242880 | tf_op jit(solution)/shard_map/all_gather | solution.py:174
  12.0 6.5 copy-start.20
  12.0 6.5 copy-start.22
  12.0 6.5 copy-start.2
  18.5 1.6 copy-start.28
  20.0 102.4 %all-gather.10.cloned.1.call-start = ((), (), s32[]{:S(2)}) async-start(), calls=%async_computation.8 | async-start | bytes 3145728 | tf_op jit(solution)/shard_map/all_gather | solution.py:182
  109.3 2.7 copy-start.10
  113.2 23.1 %all-gather.18.cloned.1.call-start = ((), (), s32[]{:S(2)}) async-start(), calls=%async_computation.19 | async-start | bytes 3145728 | tf_op jit(solution)/shard_map/all_gather | solution.py:181
  115.9 190.6 %reduce-scatter.8.cloned.1.call-start = ((), (), s32[]{:S(2)}) async-start(), calls=%async_computation.9 | async-start | bytes 5242880 | tf_op jit(solution)/shard_map/reduce_scatter | solution.py:195
  116.0 1.6 slice-start
  118.7 105.5 %copy-start.18 = (bf16[256,1024]{1,0:T(8,128)(2,1)S(1)}, bf16[256,1024]{1,0:T(8,128)(2,1)}, u32[]{:S(2)}) copy-start(bf16[256,1024]{1,0:T(8,128)(2,1)} %param.17) | copy-start | bytes 1572868
  228.8 164.3 %all-gather.12.cloned.1.call-start = ((), (), s32[]{:S(2)}) async-start(), calls=%async_computation.10 | async-start | bytes 5242880 | tf_op jit(solution)/shard_map/all_gather | solution.py:207
  308.9 3.2 copy-start.30
  311.6 174.0 %reduce-scatter.10.cloned.1.call-start = ((), (), s32[]{:S(2)}) async-start(), calls=%async_computation.11 | async-start | bytes 5242880 | tf_op jit(solution)/shard_map/reduce_scatter | solution.py:213
  400.0 3.2 copy-start.38
  410.2 160.7 %all-gather.14.cloned.1.call-start = ((), (), s32[]{:S(2)}) async-start(), calls=%async_computation.12 | async-start | bytes 5242880 | tf_op jit(solution)/shard_map/all_gather | solution.py:227
  489.5 177.9 %reduce-scatter.12.cloned.1.call-start = ((), (), s32[]{:S(2)}) async-start(), calls=%async_computation.13 | async-start | bytes 5242880 | tf_op jit(solution)/shard_map/reduce_scatter | solution.py:236
  570.9 14.8 %copy-start.35 = (bf16[1024,1024]{1,0:T(8,128)(2,1)S(1)}, bf16[1024,1024]{1,0:T(8,128)(2,1)}, u32[]{:S(2)}) copy-start(bf16[1024,1024]{1,0:T(8,128)(2,1)} %param.19) | copy-start | bytes 6291460
  583.7 2.0 copy-start.37
  592.0 75.5 %copy-start.5 = (f32[1,8,64,1024]{3,2,1,0:T(8,128)S(1)}, f32[1,8,64,1024]{3,2,1,0:T(8,128)}, u32[]{:S(2)}) copy-start(f32[1,8,64,1024]{3,2,1,0:T(8,128)} %copy-done.4) | copy-start | bytes 6291460
  592.0 165.7 %all-gather.16.cloned.1.call-start = ((), (), s32[]{:S(2)}) async-start(), calls=%async_computation.14 | async-start | bytes 5242880 | tf_op jit(solution)/shard_map/all_gather | solution.py:251
  667.4 2.4 copy-start.9
  667.4 2.4 copy-start.11
  673.7 84.0 %copy-start.19 = (bf16[256,1024]{1,0:T(8,128)(2,1)S(1)}, bf16[256,1024]{1,0:T(8,128)(2,1)}, u32[]{:S(2)}) copy-start(bf16[256,1024]{1,0:T(8,128)(2,1)} %param.17) | copy-start | bytes 1572868
  676.3 185.0 %reduce-scatter.14.cloned.1.call-start = ((), (), s32[]{:S(2)}) async-start(), calls=%async_computation.15 | async-start | bytes 3145728 | tf_op jit(solution)/shard_map/reduce_scatter | solution.py:271
  853.6 21.6 %copy-start.16 = (bf16[1,2048,256]{2,1,0:T(8,128)(2,1)S(1)}, bf16[1,2048,256]{2,1,0:T(8,128)(2,1)}, u32[]{:S(2)}) copy-start(bf16[1,2048,256]{2,1,0:T(8,128)(2,1)} %get-tuple-element.21) | copy-start | bytes 3145732
  853.7 21.6 %reduce-scatter.16.cloned.1.call-start = ((), (), s32[]{:S(2)}) async-start(), calls=%async_computation.16 | async-start | bytes 3145728 | tf_op jit(solution)/shard_map/reduce_scatter | solution.py:277
  854.4 106.6 %reduce-scatter.18.cloned.1.call-start = ((), (), s32[]{:S(2)}) async-start(), calls=%async_computation.17 | async-start | bytes 5242880 | tf_op jit(solution)/shard_map/reduce_scatter | solution.py:297
  882.8 102.8 %reduce-scatter.20.cloned.1.call-start = ((), (), s32[]{:S(2)}) async-start(), calls=%async_computation.18 | async-start | bytes 122880 | tf_op jit(solution)/shard_map/reduce_scatter | solution.py:322
  882.9 9.6 copy-start.33
  892.4 11.3 copy-start.12
  892.4 11.3 copy-start.34
  903.7 58.8 %copy-start.3 = (f32[1,8,64,1024]{3,2,1,0:T(8,128)S(1)}, f32[1,8,64,1024]{3,2,1,0:T(8,128)}, u32[]{:S(2)}) copy-start(f32[1,8,64,1024]{3,2,1,0:T(8,128)} %param.14) | copy-start | bytes 6291460
  905.8 59.9 %copy-start.17 = (bf16[1,2048,256]{2,1,0:T(8,128)(2,1)S(1)}, bf16[1,2048,256]{2,1,0:T(8,128)(2,1)}, u32[]{:S(2)}) copy-start(bf16[1,2048,256]{2,1,0:T(8,128)(2,1)} %get-tuple-element.21) | copy-start | bytes 3145732
  965.6 20.1 %copy-start.21 = (f32[8,512]{1,0:T(8,128)S(1)}, f32[8,512]{1,0:T(8,128)}, u32[]{:S(2)}) copy-start(f32[8,512]{1,0:T(8,128)} %copy-done.20) | copy-start | bytes 49156
  965.6 20.0 %copy-start.23 = (f32[8,512]{1,0:T(8,128)S(1)}, f32[8,512]{1,0:T(8,128)}, u32[]{:S(2)}) copy-start(f32[8,512]{1,0:T(8,128)} %copy-done.22) | copy-start | bytes 49156
  965.6 161.9 %all-reduce.7.cloned.1.call-start = ((), (), s32[]{:S(2)}) async-start(), calls=%async_computation.20 | async-start | bytes 18874368 | tf_op jit(solution)/shard_map/psum | solution.py:347
  989.1 1.9 copy-start.27
  1000.0 2.4 copy-start.7
  1000.0 2.6 copy-start.8
  1002.6 2.0 copy-start.25
  1127.6 5.6 copy-start.15
  1133.2 2.5 copy-start.14
  1135.7 3.1 copy-start.13
  1138.1 4.1 copy-start.1
  (6 other events, 5.3 us)
Sparse Core Ops, SparseCore 0:
  20.1 83.4 all-gather.7
  113.3 9.0 all-gather.9
  124.5 11.7 all-gather.17
  228.9 77.6 reduce-scatter.7
  311.7 81.2 all-gather.11
  410.3 75.2 reduce-scatter.9
  489.6 81.2 all-gather.13
  592.1 75.2 reduce-scatter.11
  676.4 81.2 all-gather.15
  853.8 7.5 reduce-scatter.13
  864.2 11.0 reduce-scatter.15
  882.9 78.0 reduce-scatter.17
  965.7 19.8 reduce-scatter.19
  991.0 136.5 all-reduce.6
